TPU v7x, 32 devices: a whole 2x2x4 slice. The times are simulated.
32 devices in a mesh: rep: 8 (over z, y), zero: 4 (over x, core).
Axes of the slice: x: 2, y: 2, z: 4, core: 2. Of those that a mesh axis runs over, the one named last changes fastest.
Arguments:
- tokens: bfloat16 [12288, 1280], P(('rep', 'zero')), may hold values from -6 to 6
- cotangent: bfloat16 [12288, 1280], P(('rep', 'zero')), may hold values from -6 to 6
- weights: bfloat16 [1280, 6, 1280], P('zero')
- vectors: bfloat16 [5, 1280], P(None, 'zero')
- error: float32 [10240, 6, 1280], P(('rep', 'zero'))
- previous_right_factors: float32 [6, 1280, 32], P(None, None, 'zero'), may hold values from -6 to 6
- momentum: float32 [1280, 6, 1280], P('zero', None, 'rep')
- vec_momentum: float32 [5, 1280], P(None, 'zero')
- prompt_len: int32 [8], P('rep'), may hold values from 512 to 1024, as said below
Outputs:
- result: bfloat16 [12288, 1280], P(('rep', 'zero'))
- grad_tokens: float32 [12288, 1280], P(('rep', 'zero'))
- grad_weights: float32 [1280, 6, 1280], P('zero', None, 'rep')
- grad_vectors: float32 [5, 1280], P(None, 'zero')
- new_error: float32 [10240, 6, 1280], P(('rep', 'zero'))
- fresh_right_factors: float32 [6, 1280, 32], P(None, None, 'zero')
- new_momentum: float32 [1280, 6, 1280], P('zero', None, 'rep')
- new_vec_momentum: float32 [5, 1280], P(None, 'zero')
- update_weights: float32 [1280, 6, 1280], P('zero', None, 'rep')
- update_vectors: float32 [5, 1280], P(None, 'zero')
Inputs may be any that keep to these rules, and one draw needn't show every extreme that they name: `prompt_len`: valid prompt rows of a group; the other prompt rows of its 1024 are padding.
All inputs are finite; a program needn't handle non-finite values.
Results may differ from a plain program's by a relative error of at most 0.028.
Values may be sent and summed in bfloat16 or wider, within the bound.
No kernel may reach another device: no remote copies, remote signals or barrier semaphores. Data moves between devices by JAX's collectives and lax.ppermute only.
A program may use at most 320 MiB of HBM per device.

v0:
```python
import math
import jax
import jax.numpy as jnp
from jax import lax
from jax.sharding import PartitionSpec as P

HEADS = 16
PROMPT = 1024
EPS = 1e-06
MU = 0.9
LOG2E = 1.442695041
NEG = -1e30
PRECISION_HIGH = lax.Precision.HIGHEST


def rms_scale(field):
    return lax.rsqrt(jnp.mean(field * field, axis=-1, keepdims=True) + EPS)


def norm_back(field, scale, gain_vec, grad_in):
    weighted = grad_in * gain_vec
    inner = jnp.mean(field * weighted, axis=-1, keepdims=True)
    return scale * weighted - field * (scale * scale * scale) * inner


def orthonormal(factor):
    columns = []
    for col_index in range(factor.shape[-1]):
        column = factor[..., col_index]
        for earlier in columns:
            column = column - jnp.sum(earlier * column, axis=-2, keepdims=True) * earlier
        column = column * lax.rsqrt(jnp.sum(column * column, axis=-2, keepdims=True) + EPS)
        columns.append(column)
    return jnp.stack(columns, axis=-1)


def on_device(
    tokens,
    cotangent,
    weights,
    vectors,
    error,
    previous_right_factors,
    momentum,
    vec_momentum,
    prompt_len,
):
    f32 = jnp.float32
    bf16 = jnp.bfloat16
    zero_index = lax.axis_index("zero")
    rep_index = lax.axis_index("rep")
    zero_count = lax.axis_size("zero")
    rep_count = lax.axis_size("rep")
    tok_rows, feat_width = tokens.shape
    head_dim = feat_width // HEADS
    prompt_rows = PROMPT // zero_count
    prompt_valid = prompt_len[0]
    full_w, full_v = (
        lax.all_gather(weights, "zero", axis=0, tiled=True),
        lax.all_gather(vectors, "zero", axis=1, tiled=True),
    )
    vec_float = full_v.astype(f32)
    gain_one = vec_float[0]
    gain_two = vec_float[1]
    bias_one = vec_float[2]
    bias_two = vec_float[3]
    scale_raw = vec_float[4]
    tok_float = tokens.astype(f32)
    scale_one = rms_scale(tok_float)
    normed_one = (tok_float * scale_one * gain_one).astype(bf16)
    projected = jnp.einsum("ti,omi->mto", normed_one, full_w[:, 0:3, :], preferred_element_type=f32)
    query = projected[0]
    key_low = projected[1].astype(bf16)
    value_low = projected[2].astype(bf16)
    scale_const = LOG2E / math.sqrt(head_dim)
    query_scale = scale_const * jax.nn.softplus(scale_raw)
    scaled = (query * query_scale).astype(bf16)
    key_far, value_far = (
        lax.all_gather(key_low[:prompt_rows], "zero", axis=0, tiled=True),
        lax.all_gather(value_low[:prompt_rows], "zero", axis=0, tiled=True),
    )
    key_rows = jnp.concatenate([key_far, key_low[prompt_rows:]], axis=0)
    value_rows = jnp.concatenate([value_far, value_low[prompt_rows:]], axis=0)
    key_count = key_rows.shape[0]
    q_row = lax.broadcasted_iota(jnp.int32, (tok_rows, key_count), 0)
    k_col = lax.broadcasted_iota(jnp.int32, (tok_rows, key_count), 1)
    q_prompt = q_row < prompt_rows
    q_pos = zero_index * prompt_rows + q_row
    k_prompt = k_col < PROMPT
    see_prompt = k_prompt & (k_col < prompt_valid) & (jnp.logical_not(q_prompt) | (k_col <= q_pos))
    see_cont = (
        jnp.logical_not(k_prompt)
        & jnp.logical_not(q_prompt)
        & (k_col - PROMPT <= q_row - prompt_rows)
    )
    allowed = see_prompt | see_cont
    q_heads = scaled.reshape(tok_rows, HEADS, head_dim)
    k_heads = key_rows.reshape(key_count, HEADS, head_dim)
    v_heads = value_rows.reshape(key_count, HEADS, head_dim)

    def masked_scores():
        raw_scores = jnp.einsum("thd,khd->htk", q_heads, k_heads, preferred_element_type=f32)
        return jnp.where(allowed[None], raw_scores, NEG)

    masked = masked_scores()
    row_top = jnp.max(masked, axis=-1, keepdims=True)
    log_total = row_top + jnp.log(jnp.sum(jnp.exp(masked - row_top), axis=-1, keepdims=True))
    probs = jnp.exp(masked - log_total)
    attended = (
        jnp.einsum("htk,khd->thd", probs.astype(bf16), v_heads, preferred_element_type=f32)
        .reshape(tok_rows, feat_width)
        .astype(bf16)
    )
    branch = jnp.einsum("ti,oi->to", attended, full_w[:, 3, :], preferred_element_type=f32)
    hidden = tok_float + branch
    scale_two = rms_scale(hidden)
    normed_two = (hidden * scale_two * gain_two).astype(bf16)
    upper = (
        jnp.einsum("ti,oi->to", normed_two, full_w[:, 4, :], preferred_element_type=f32) + bias_one
    )
    activ = jax.nn.silu(upper).astype(bf16)
    output = jnp.einsum("ti,oi->to", activ, full_w[:, 5, :], preferred_element_type=f32) + bias_two
    result = (hidden + output).astype(bf16)
    back_w = lax.all_gather(weights, "zero", axis=0, tiled=True)
    grad_out = cotangent.astype(f32)
    grad_f = grad_out.astype(bf16)
    grad_act = jnp.einsum("to,oi->ti", grad_f, back_w[:, 5, :], preferred_element_type=f32)
    gate_sig = jax.nn.sigmoid(upper)
    grad_up = (grad_act * gate_sig * (1.0 + upper * (1.0 - gate_sig))).astype(bf16)
    grad_n2 = jnp.einsum("to,oi->ti", grad_up, back_w[:, 4, :], preferred_element_type=f32)
    grad_gain_two = jnp.sum(grad_n2 * hidden * scale_two, axis=0)
    grad_hidden = grad_out + norm_back(hidden, scale_two, gain_two, grad_n2)
    grad_branch = grad_hidden.astype(bf16)
    grad_att = jnp.einsum(
        "to,oi->ti", grad_branch, back_w[:, 3, :], preferred_element_type=f32
    ).astype(bf16)
    grad_att_heads = grad_att.reshape(tok_rows, HEADS, head_dim)
    probs_again = jnp.exp(masked_scores() - log_total)
    grad_probs = jnp.einsum("thd,khd->htk", grad_att_heads, v_heads, preferred_element_type=f32)
    delta = jnp.sum(probs_again * grad_probs, axis=-1, keepdims=True)
    grad_scores = (probs_again * (grad_probs - delta)).astype(bf16)
    grad_values = jnp.einsum(
        "htk,thd->khd", probs_again.astype(bf16), grad_att_heads, preferred_element_type=f32
    ).reshape(key_count, feat_width)
    grad_keys = jnp.einsum(
        "htk,thd->khd", grad_scores, q_heads, preferred_element_type=f32
    ).reshape(key_count, feat_width)
    grad_sq = jnp.einsum("htk,khd->thd", grad_scores, k_heads, preferred_element_type=f32).reshape(
        tok_rows, feat_width
    )
    own_keys, own_values = (
        lax.psum_scatter(
            grad_keys[:PROMPT].astype(jnp.bfloat16), "zero", scatter_dimension=0, tiled=True
        ).astype(jnp.float32),
        lax.psum_scatter(
            grad_values[:PROMPT].astype(jnp.bfloat16), "zero", scatter_dimension=0, tiled=True
        ).astype(jnp.float32),
    )
    grad_key = jnp.concatenate([own_keys, grad_keys[PROMPT:]], axis=0).astype(bf16)
    grad_value = jnp.concatenate([own_values, grad_values[PROMPT:]], axis=0).astype(bf16)
    grad_query = (grad_sq * query_scale).astype(bf16)
    grad_scale_raw = jnp.sum(grad_sq * query, axis=0) * scale_const * jax.nn.sigmoid(scale_raw)
    grad_proj = jnp.stack([grad_query, grad_key, grad_value], axis=0)
    grad_n1 = jnp.einsum("mto,omi->ti", grad_proj, back_w[:, 0:3, :], preferred_element_type=f32)
    grad_gain_one = jnp.sum(grad_n1 * tok_float * scale_one, axis=0)
    grad_tokens = grad_hidden + norm_back(tok_float, scale_one, gain_one, grad_n1)
    grad_stack = jnp.stack([grad_query, grad_key, grad_value, grad_branch, grad_up, grad_f], axis=0)
    input_stack = jnp.stack(
        [normed_one, normed_one, normed_one, attended, normed_two, activ], axis=0
    )
    grad_block = lax.psum_scatter(
        jnp.einsum("mto,mti->omi", grad_stack, input_stack, preferred_element_type=f32).astype(
            jnp.bfloat16
        ),
        "zero",
        scatter_dimension=0,
        tiled=True,
    ).astype(jnp.float32)
    vec_terms = jnp.stack(
        [
            grad_gain_one,
            grad_gain_two,
            jnp.sum(grad_up.astype(f32), axis=0),
            jnp.sum(grad_f.astype(f32), axis=0),
            grad_scale_raw,
        ],
        axis=0,
    )
    vec_block = lax.psum_scatter(vec_terms, "zero", scatter_dimension=1, tiled=True)
    combined_result = grad_block + error
    local_left_factor = jnp.einsum(
        "edn,dnw->edw", combined_result, previous_right_factors, precision=PRECISION_HIGH
    )
    vec_total = lax.psum(vec_block, "rep")
    left_parts = []
    right_parts = []
    for mat_index in range(combined_result.shape[1]):
        left_sum = lax.psum(local_left_factor[:, mat_index], "rep")
        left_ortho = orthonormal(left_sum[:, None, :] / rep_count)[:, 0, :]
        right_term = jnp.einsum(
            "oi,or->ir", combined_result[:, mat_index], left_ortho, precision=PRECISION_HIGH
        )
        right_parts.append(lax.psum(right_term.astype(jnp.bfloat16), "rep").astype(jnp.float32))
        left_parts.append(left_ortho)
    orthogonalized = jnp.stack(left_parts, axis=1)
    right_total = jnp.stack(right_parts, axis=0)
    fresh_right_factors = right_total / rep_count
    approximation = jnp.einsum(
        "upt,pqt->upq", orthogonalized, fresh_right_factors, precision=PRECISION_HIGH
    )
    new_error = combined_result - approximation
    rep_width = feat_width // rep_count
    grad_weights = lax.dynamic_slice_in_dim(approximation, rep_index * rep_width, rep_width, 2)
    step_rate = 0.03 / math.sqrt(zero_count * tok_rows)
    new_momentum = MU * momentum + grad_weights
    update_weights = -step_rate * new_momentum
    grad_vectors = vec_total / rep_count
    new_vec_momentum = MU * vec_momentum + grad_vectors
    update_vectors = -step_rate * new_vec_momentum
    return (
        result,
        grad_tokens,
        grad_weights,
        grad_vectors,
        new_error,
        fresh_right_factors,
        new_momentum,
        new_vec_momentum,
        update_weights,
        update_vectors,
    )


def solution(mesh):
    in_specs = (
        P(("rep", "zero"), None),
        P(("rep", "zero"), None),
        P("zero", None, None),
        P(None, "zero"),
        P(("rep", "zero"), None, None),
        P(None, None, "zero"),
        P("zero", None, "rep"),
        P(None, "zero"),
        P("rep"),
    )
    out_specs = (
        P(("rep", "zero"), None),
        P(("rep", "zero"), None),
        P("zero", None, "rep"),
        P(None, "zero"),
        P(("rep", "zero"), None, None),
        P(None, None, "zero"),
        P("zero", None, "rep"),
        P(None, "zero"),
        P("zero", None, "rep"),
        P(None, "zero"),
    )
    return jax.shard_map(
        on_device, mesh=mesh, in_specs=in_specs, out_specs=out_specs, check_vma=False
    )
```

profile of v0, /device:TPU:0, one launch (start us, length us, event | category | flops | bytes accessed | tf_op | source)
XLA Modules:
  0.0 1215.3 jit_solution(3644075702543074997)
XLA Ops:
  15.9 120.7 %all-gather.7.cloned.1.call-done = bf16[1280,6,1280]{2,0,1:T(8,128)(2,1)} async-done(((bf16[320,6,1280]{2,0,1:T(8,128)(2,1)}), bf16[1280,6,1280]{2,0,1:T(8,128)(2,1)}) %all-gather.7.cloned.1.call-update) | async-done | bytes 19660816 | tf_op jit(solution)/shard_map/all_gather | solution.py:59
  163.3 12.1 all-gather.9.cloned.1.call-done
  175.4 27.7 %all-gather.11.cloned.1.call-done = bf16[1,1024,1280]{2,1,0:T(8,128)(2,1)} async-done(((bf16[1,256,1280]{2,1,0:T(8,128)(2,1)}), bf16[1,1024,1280]{2,1,0:T(8,128)(2,1)}) %all-gather.11.cloned.1.call-update) | async-done | bytes 2621456 | tf_op jit(solution)/shard_map/all_gather | solution.py:79
  218.6 13.1 %select_reduce_fusion = (f32[16,384]{1,0:T(8,128)S(1)}, f32[16,384,1152]{2,1,0:T(8,128)}) fusion(pred[384,1152]{1,0:T(8,128)(4,1)} %fusion.50, bf16[1152,16,80]{0,2,1:T(8,128)(2,1)} %bitcast.662, f32[384,16,80]{0,2,1:T(8,128)S(1)} %bitcast.659, f32[16,80]{1,0:T(8,128)S(1)} %mul.16566), kind=kOutput, calls=%fused_computation.5 | convolution fusion | flops 1147594752 | bytes 33698816 | tf_op jit(solution)/shard_map/thd,khd->htk/dot_general | solution.py:102
  231.6 13.7 %exponential_reduce_fusion = f32[16,384]{1,0:T(8,128)S(1)} fusion(f32[16,384,1152]{2,1,0:T(8,128)} %get-tuple-element.459, f32[16,384]{1,0:T(8,128)S(1)} %get-tuple-element.458, pred[384,1152]{1,0:T(8,128)(4,1)S(1)} %copy-done.3), kind=kLoop, calls=%fused_computation.3 | loop fusion | flops 21227520 | bytes 28803072 | tf_op jit(solution)/shard_map/reduce_sum | solution.py:107
  245.3 13.1 %fusion.51 = bf16[16,80,384]{2,1,0:T(8,128)(2,1)} fusion(bf16[1152,16,80]{0,2,1:T(8,128)(2,1)S(1)} %bitcast.665, f32[16,384,1152]{2,1,0:T(8,128)} %get-tuple-element.459, f32[16,384]{1,0:T(8,128)S(1)} %log_add_fusion, pred[384,1152]{1,0:T(8,128)(4,1)S(1)} %copy-done.3), kind=kOutput, calls=%fused_computation.96 | convolution fusion | flops 1154187264 | bytes 32710656 | tf_op jit(solution)/shard_map/htk,khd->thd/dot_general | solution.py:110
  289.8 24.5 %multiply_reduce_fusion = (f32[16,384]{1,0:T(8,128)S(1)}, f32[16,384,1152]{2,1,0:T(8,128)}) fusion(f32[16,384,1152]{2,1,0:T(8,128)} %get-tuple-element.459, f32[16,384]{1,0:T(8,128)S(1)} %log_add_fusion, pred[384,1152]{1,0:T(8,128)(4,1)} %fusion.50, bf16[384,16,80]{0,2,1:T(8,128)(2,1)} %bitcast.669, bf16[1152,16,80]{0,2,1:T(8,128)(2,1)} %bitcast.664), kind=kOutput, calls=%fused_computation.1 | convolution fusion | flops 1160767488 | bytes 61046784 | tf_op jit(solution)/shard_map/thd,khd->htk/dot_general | solution.py:139
  314.3 23.7 %multiply_convert_fusion = bf16[16,384,1152]{2,1,0:T(8,128)(2,1)} fusion(f32[16,384,1152]{2,1,0:T(8,128)} %get-tuple-element.464, f32[16,384,1152]{2,1,0:T(8,128)} %get-tuple-element.459, f32[16,384]{1,0:T(8,128)S(1)} %get-tuple-element.463, f32[16,384]{1,0:T(8,128)S(1)} %log_add_fusion, pred[384,1152]{1,0:T(8,128)(4,1)} %fusion.50), kind=kLoop, calls=%fused_computation | loop fusion | flops 35389440 | bytes 71270400 | tf_op jit(solution)/shard_map/convert_element_type | solution.py:141
  354.1 14.2 %fusion.9 = bf16[1152,16,80]{0,2,1:T(8,128)(2,1)S(1)} fusion(bf16[384,16,80]{0,2,1:T(8,128)(2,1)} %bitcast.670, f32[16,384,1152]{2,1,0:T(8,128)} %get-tuple-element.459, f32[16,384]{1,0:T(8,128)S(1)} %log_add_fusion, pred[384,1152]{1,0:T(8,128)(4,1)} %fusion.50), kind=kOutput, calls=%fused_computation.23 | convolution fusion | flops 1155170304 | bytes 32710656 | tf_op jit(solution)/shard_map/htk,thd->khd/dot_general | solution.py:142
  380.8 11.7 fusion.44
  401.2 24.4 %reduce-scatter.11.cloned.1.call-done = bf16[256,1280]{1,0:T(8,128)(2,1)} async-done(((bf16[1024,1280]{1,0:T(8,128)(2,1)}), bf16[256,1280]{1,0:T(8,128)(2,1)}) %reduce-scatter.11.cloned.1.call-update) | async-done | bytes 655376 | tf_op jit(solution)/shard_map/reduce_scatter | solution.py:155
  442.1 17.9 %convolution_convert_fusion = bf16[6,1280,1280]{2,1,0:T(8,128)(2,1)} fusion(bf16[6,384,1280]{2,1,0:T(8,128)(2,1)} %get-tuple-element.466, bf16[6,384,1280]{2,1,0:T(8,128)(2,1)} %bitcast_dynamic-update-slice_fusion), kind=kOutput, calls=%fused_computation.4 | convolution fusion | flops 7559577600 | bytes 31457280 | tf_op jit(solution)/shard_map/mto,mti->omi/dot_general | solution.py:172
  460.0 26.4 %copy.101 = bf16[1280,7680]{1,0:T(8,128)(2,1)} copy(bf16[1280,7680]{0,1:T(8,128)(2,1)} %bitcast.668) | data formatting | bytes 39321600
  497.8 131.3 %reduce-scatter.13.cloned.1.call-done = bf16[320,7680]{1,0:T(8,128)(2,1)} async-done(((bf16[1280,7680]{1,0:T(8,128)(2,1)}), bf16[320,7680]{1,0:T(8,128)(2,1)}) %reduce-scatter.13.cloned.1.call-update) | async-done | bytes 4915216
  656.0 10.7 convolution_bitcast_fusion
  671.0 68.0 %all-reduce.5.cloned.1.call-done = (f32[320,8]{0,1:T(8,128)}, f32[320,8]{0,1:T(8,128)}, f32[320,8]{0,1:T(8,128)}, f32[320,8]{0,1:T(8,128)}, f32[320,8]{0,1:T(8,128)}, /*index=5*/f32[320,8]{0,1:T(8,128)}, f32[5,320]{1,0:T(8,128)}) async-done(((f32[320,8]{0,1:T(8,128)}, f32[320,8]{0,1:T(8,128)}, f32[320,8]{0,1:T(8,128)}, f32[320,8]{0,1:T(8,128)}, f32[320,8]{0,1:T(8,128)}, /*index=5*/f32[320,8]{0,1:T(8,128)}, ...) | async-done | bytes 67856 | tf_op jit(solution)/shard_map/psum | solution.py:198
  780.5 17.7 %subtract_multiply_fusion.35 = (f32[320,1,1]{0,2,1:T(1,128)S(1)}, f32[320,1,1]{0,2,1:T(1,128)S(1)}, f32[320,1,1]{0,2,1:T(1,128)S(1)}, f32[320,1,1]{0,2,1:T(1,128...) fusion(f32[320,1,1]{0,2,1:T(1,128)S(1)} %get-tuple-element.437, ...), kind=kLoop, calls=%fused_computation.622 | loop fusion | flops 20160 | bytes 19340 | tf_op jit(solution)/shard_map/mul | solution.py:32
  842.7 17.6 %subtract_multiply_fusion.28 = (f32[320,1,1]{0,2,1:T(1,128)S(1)}, f32[320,1,1]{0,2,1:T(1,128)S(1)}, f32[320,1,1]{0,2,1:T(1,128)S(1)}, f32[320,1,1]{0,2,1:T(1,128...) fusion(f32[320,1,1]{0,2,1:T(1,128)S(1)} %get-tuple-element.404, ...), kind=kLoop, calls=%fused_computation.566 | loop fusion | flops 20160 | bytes 19340 | tf_op jit(solution)/shard_map/mul | solution.py:32
  904.0 17.6 %subtract_multiply_fusion.21 = (f32[320,1,1]{0,2,1:T(1,128)S(1)}, f32[320,1,1]{0,2,1:T(1,128)S(1)}, f32[320,1,1]{0,2,1:T(1,128)S(1)}, f32[320,1,1]{0,2,1:T(1,128...) fusion(f32[320,1,1]{0,2,1:T(1,128)S(1)} %get-tuple-element.371, ...), kind=kLoop, calls=%fused_computation.510 | loop fusion | flops 20160 | bytes 19340 | tf_op jit(solution)/shard_map/mul | solution.py:32
  965.4 17.6 %subtract_multiply_fusion.14 = (f32[320,1,1]{0,2,1:T(1,128)S(1)}, f32[320,1,1]{0,2,1:T(1,128)S(1)}, f32[320,1,1]{0,2,1:T(1,128)S(1)}, f32[320,1,1]{0,2,1:T(1,128...) fusion(f32[320,1,1]{0,2,1:T(1,128)S(1)} %get-tuple-element.338, ...), kind=kLoop, calls=%fused_computation.454 | loop fusion | flops 20160 | bytes 19340 | tf_op jit(solution)/shard_map/mul | solution.py:32
  1026.8 17.6 %subtract_multiply_fusion.7 = (f32[320,1,1]{0,2,1:T(1,128)S(1)}, f32[320,1,1]{0,2,1:T(1,128)S(1)}, f32[320,1,1]{0,2,1:T(1,128)S(1)}, f32[320,1,1]{0,2,1:T(1,128)...) fusion(f32[320,1,1]{0,2,1:T(1,128)S(1)} %get-tuple-element.305, ...), kind=kLoop, calls=%fused_computation.398 | loop fusion | flops 20160 | bytes 19340 | tf_op jit(solution)/shard_map/mul | solution.py:32
  1088.3 17.5 %subtract_multiply_fusion = (f32[320,1,1]{0,2,1:T(1,128)S(1)}, f32[320,1,1]{0,2,1:T(1,128)S(1)}, f32[320,1,1]{0,2,1:T(1,128)S(1)}, f32[320,1,1]{0,2,1:T(1,128)S(...) fusion(f32[320,1,1]{0,2,1:T(1,128)S(1)} %get-tuple-element.272, f32[]{:T(128)S(6)} %rsqrt.263, ...), kind=kLoop, calls=%fused_computation.342 | loop fusion | flops 20160 | bytes 19340 | tf_op jit(solution)/shard_map/mul | solution.py:32
  1109.5 71.6 %all-reduce.7.cloned.1.call-done = (bf16[1,1280,8]{1,2,0:T(8,128)(2,1)}, bf16[1,1280,8]{1,2,0:T(8,128)(2,1)}, bf16[1,1280,8]{1,2,0:T(8,128)(2,1)}, bf16[1,1280,8...) async-done(((bf16[1,1280,8]{1,2,0:T(8,128)(2,1)}, bf16[1,1280,8]{1,2,0:T(8,128)(2,1)}, bf16[1,1280,8]{1,2,0:T(8,128)(2,1)}, ...) | async-done | bytes 122896 | tf_op jit(solution)/shard_map/psum | solution.py:203
  1185.5 12.8 %bitcast_subtract_fusion = (f32[320,6,1280]{2,0,1:T(8,128)}, f32[6,1280,320]{1,2,0:T(8,128)S(1)}) fusion(f32[320,6,1280]{2,0,1:T(8,128)} %convert_add_fusion, f32[6,1280,8]{1,2,0:T(8,128)S(1)} %convert_multiply_fusion.5, f32[320,6,8]{0,2,1:T(8,128)S(1)} %constant_dynamic-update-slice_fusion.8), kind=kOutput, calls=%fused_computation.7 | convolution fusion | flops 238387200 | bytes 29798400 | tf_op jit(solution)/shard_map/upt,pqt->upq/dot_general | solution.py:208
  (304 shorter events, 424.6 us)
Async XLA Ops:
  7.2 648.8 %copy-start = (f32[6,1280,8]{1,2,0:T(8,128)S(1)}, f32[6,1280,8]{1,2,0:T(8,128)}, u32[]{:S(2)}) copy-start(f32[6,1280,8]{1,2,0:T(8,128)} %param.14) | copy-start | bytes 737284
  7.2 129.4 %all-gather.7.cloned.1.call-start = ((), (), s32[]{:S(2)}) async-start(), calls=%async_computation.4 | async-start | bytes 24576000 | tf_op jit(solution)/shard_map/all_gather | solution.py:59
  7.9 167.5 %all-gather.9.cloned.1.call-start = ((), (), s32[]{:S(2)}) async-start(), calls=%async_computation.7 | async-start | bytes 3276800 | tf_op jit(solution)/shard_map/all_gather | solution.py:80
  14.3 132.7 %copy-start.25 = (f32[1280,5]{0,1:T(8,128)}, f32[1280,5]{0,1:T(8,128)S(1)}, u32[]{:S(2)}) copy-start(f32[1280,5]{0,1:T(8,128)S(1)} %reshape.8102) | copy-start | bytes 76804
  15.0 136.4 %copy-start.26 = (f32[1280]{0:T(1024)}, f32[1280]{0:T(1024)S(1)}, u32[]{:S(2)}) copy-start(f32[1280]{0:T(1024)S(1)} %get-tuple-element.55) | copy-start | bytes 15364
  15.0 138.7 %copy-start.22 = (f32[1280]{0:T(1024)}, f32[1280]{0:T(1024)S(1)}, u32[]{:S(2)}) copy-start(f32[1280]{0:T(1024)S(1)} %get-tuple-element.58) | copy-start | bytes 15364
  15.8 137.9 %copy-start.28 = (f32[384]{0:T(512)}, f32[384]{0:T(512)S(1)}, u32[]{:S(2)}) copy-start(f32[384]{0:T(512)S(1)} %get-tuple-element.453) | copy-start | bytes 4612
  149.7 53.4 %all-gather.11.cloned.1.call-start = ((), (), s32[]{:S(2)}) async-start(), calls=%async_computation.8 | async-start | bytes 3276800 | tf_op jit(solution)/shard_map/all_gather | solution.py:79
  150.5 248.2 %reduce-scatter.9.cloned.1.call-start = ((), (), s32[]{:S(2)}) async-start(), calls=%async_computation.5 | async-start | bytes 3276800 | tf_op jit(solution)/shard_map/reduce_scatter | solution.py:152
  231.6 13.7 %copy-start.2 = (bf16[1152,1280]{0,1:T(8,128)(2,1)S(1)}, bf16[1152,1280]{0,1:T(8,128)(2,1)}, u32[]{:S(2)}) copy-start(bf16[1152,1280]{0,1:T(8,128)(2,1)} %copy.80) | copy-start | bytes 8847364
  264.9 16.4 %copy-start.9 = (f32[384,1280]{1,0:T(8,128)}, f32[384,1280]{1,0:T(8,128)S(1)}, u32[]{:S(2)}) copy-start(f32[384,1280]{1,0:T(8,128)S(1)} %get-tuple-element.461) | copy-start | bytes 5898244
  354.0 71.6 %reduce-scatter.11.cloned.1.call-start = ((), (), s32[]{:S(2)}) async-start(), calls=%async_computation.6 | async-start | bytes 3276800 | tf_op jit(solution)/shard_map/reduce_scatter | solution.py:155
  376.2 119.9 %reduce-scatter.15.cloned.1.call-start = ((), (), s32[]{:S(2)}) async-start(), calls=%async_computation.10 | async-start | bytes 819200
  397.3 28.3 %copy-start.14 = (bf16[1,128,1280]{2,1,0:T(8,128)(2,1)S(1)}, bf16[1,128,1280]{2,1,0:T(8,128)(2,1)}, u32[]{:S(2)}) copy-start(bf16[1,128,1280]{2,1,0:T(8,128)(2,1)} %copy.88) | copy-start | bytes 983044
  398.7 29.2 %copy-start.6 = (f32[384,1280]{1,0:T(8,128)S(1)}, f32[384,1280]{1,0:T(8,128)}, u32[]{:S(2)}) copy-start(f32[384,1280]{1,0:T(8,128)} %copy-done.5) | copy-start | bytes 5898244
  442.1 187.0 %reduce-scatter.13.cloned.1.call-start = ((), (), s32[]{:S(2)}) async-start(), calls=%async_computation.9 | async-start | bytes 24576000
  486.4 252.5 %all-reduce.5.cloned.1.call-start = ((), (), s32[]{:S(2)}) async-start(), calls=%async_computation.11 | async-start | bytes 172032 | tf_op jit(solution)/shard_map/psum | solution.py:198
  667.3 513.8 %all-reduce.7.cloned.1.call-start = ((), (), s32[]{:S(2)}) async-start(), calls=%async_computation.12 | async-start | bytes 245760 | tf_op jit(solution)/shard_map/psum | solution.py:203
  739.0 124.4 %copy-start.34 = (f32[320,8]{0,1:T(8,128)S(1)}, f32[320,8]{0,1:T(8,128)}, u32[]{:S(2)}) copy-start(f32[320,8]{0,1:T(8,128)} %get-tuple-element.223) | copy-start | bytes 30724
  798.1 126.5 %copy-start.33 = (f32[320,8]{0,1:T(8,128)S(1)}, f32[320,8]{0,1:T(8,128)}, u32[]{:S(2)}) copy-start(f32[320,8]{0,1:T(8,128)} %get-tuple-element.224) | copy-start | bytes 30724
  860.3 125.8 %copy-start.32 = (f32[320,8]{0,1:T(8,128)S(1)}, f32[320,8]{0,1:T(8,128)}, u32[]{:S(2)}) copy-start(f32[320,8]{0,1:T(8,128)} %get-tuple-element.225) | copy-start | bytes 30724
  921.6 125.8 %copy-start.31 = (f32[320,8]{0,1:T(8,128)S(1)}, f32[320,8]{0,1:T(8,128)}, u32[]{:S(2)}) copy-start(f32[320,8]{0,1:T(8,128)} %get-tuple-element.226) | copy-start | bytes 30724
  983.0 125.8 %copy-start.35 = (f32[5,320]{1,0:T(8,128)S(1)}, f32[5,320]{1,0:T(8,128)}, u32[]{:S(2)}) copy-start(f32[5,320]{1,0:T(8,128)} %param.16) | copy-start | bytes 19204
  983.1 125.8 %copy-start.36 = (f32[5,320]{1,0:T(8,128)S(1)}, f32[5,320]{1,0:T(8,128)}, u32[]{:S(2)}) copy-start(f32[5,320]{1,0:T(8,128)} %get-tuple-element.227) | copy-start | bytes 19204
  (29 other events, 137.0 us)
Sparse Core Ops, SparseCore 0:
  9.6 126.9 all-gather.6
  149.9 25.5 all-gather.8
  177.6 25.5 all-gather.10
  354.1 34.4 reduce-scatter.8
  391.1 34.5 reduce-scatter.10
  442.2 22.4 reduce-scatter.14
  486.6 142.4 reduce-scatter.12
  667.5 71.4 all-reduce.4
  1109.6 71.4 all-reduce.6
where the time goes:
time: 1230 us; the launch traced here: 1220 us
  waiting for transfers between devices  457 us (37%)
  other arithmetic  393 us (32%)
  matrix products  192 us (16%)
  local copies, waits for them, and re-layouts  118 us (10%)
  between operations  47.3 us (4%)
    reduce_sum x60, other arithmetic, orthonormal(): jnp.sum(earlier * column, axis=-2, keepdims=True) * earlier  164 us
    unnamed x11, waiting for transfers between devices  133 us
    all_gather x1, waiting for transfers between devices, on_device(): lax.all_gather(weights, 'zero', axis=0, tiled=True)  121 us
    mul x6, other arithmetic, orthonormal(): column * lax.rsqrt(jnp.sum(column * column, axis=-2, keepdims=True) + EPS)  106 us
    psum x1, waiting for transfers between devices, on_device(): lax.psum(right_term.astype(jnp.bfloat16), 'rep').astype(jnp.float32)  71.6 us
    psum x1, waiting for transfers between devices, on_device(): left_sum = lax.psum(local_left_factor[:, mat_index], 'rep')  68 us
    unnamed x106, local copies, waits for them, and re-layouts  62 us
    reduce_sum x30, other arithmetic, orthonormal(): jnp.sum(column * column, axis=-2, keepdims=True) + EPS  49.2 us
  transfers between devices with their start and end apart: 9, of which 7 were waited for; matrix products, arithmetic and copies ran while one was open for 9% of the time, Pallas kernels for 0%

commit v1 on v0

--- a/solution.py
+++ b/solution.py
@@ -200,7 +200,11 @@
         right_term = jnp.einsum(
             "oi,or->ir", combined_result[:, mat_index], left_ortho, precision=PRECISION_HIGH
         )
-        right_parts.append(lax.psum(right_term.astype(jnp.bfloat16), "rep").astype(jnp.float32))
+        right_parts.append(
+            jnp.sum(lax.all_gather(right_term.astype(jnp.bfloat16), "rep"), axis=0).astype(
+                jnp.float32
+            )
+        )
         left_parts.append(left_ortho)
     orthogonalized = jnp.stack(left_parts, axis=1)
     right_total = jnp.stack(right_parts, axis=0)

time: 1230 us -> 1330 us (1.081)
  blocking collectives: 6.25 us -> 190 us
  waiting for transfers between devices: 457 us -> 386 us
    all_gather x0 -> x6, blocking collectives: none -> 184 us  [on_device(): lax.all_gather(right_term.astype(jnp.bfloat16), 'rep')]
    psum x1 -> x0, waiting for transfers between devices: 71.6 us -> none  [on_device(): lax.psum(right_term.astype(jnp.bfloat16), 'rep').astype(jnp.float32)]
    unnamed x11 -> x10, waiting for transfers between devices: 133 us -> 133 us
  transfers between devices with their start and end apart: 9 -> 8, of which waited for: 7 -> 6; matrix products, arithmetic and copies ran while one was open for 9% -> 9% of each run, Pallas kernels for 0% -> 0%
where the time goes in v1:
time: 1330 us; the launch traced here: 1320 us
  other arithmetic  392 us (29%)
  waiting for transfers between devices  386 us (29%)
  blocking collectives  190 us (14%)
  matrix products  188 us (14%)
  local copies, waits for them, and re-layouts  114 us (9%)
  between operations  48.3 us (4%)
    all_gather x6, blocking collectives, on_device(): lax.all_gather(right_term.astype(jnp.bfloat16), 'rep')  184 us
    reduce_sum x60, other arithmetic, orthonormal(): jnp.sum(earlier * column, axis=-2, keepdims=True) * earlier  163 us
    unnamed x10, waiting for transfers between devices  133 us
    all_gather x1, waiting for transfers between devices, on_device(): lax.all_gather(weights, 'zero', axis=0, tiled=True)  121 us
    mul x6, other arithmetic, orthonormal(): column * lax.rsqrt(jnp.sum(column * column, axis=-2, keepdims=True) + EPS)  106 us
    psum x1, waiting for transfers between devices, on_device(): left_sum = lax.psum(local_left_factor[:, mat_index], 'rep')  68.3 us
    unnamed x106, local copies, waits for them, and re-layouts  58.4 us
    reduce_sum x30, other arithmetic, orthonormal(): jnp.sum(column * column, axis=-2, keepdims=True) + EPS  48.9 us
  transfers between devices with their start and end apart: 8, of which 6 were waited for; matrix products, arithmetic and copies ran while one was open for 9% of the time, Pallas kernels for 0%

profile of v1, /device:TPU:0, one launch (start us, length us, event | category | flops | bytes accessed | tf_op | source)
XLA Modules:
  0.0 1319.5 jit_solution(16348582098666399118)
XLA Ops:
  15.9 120.7 %all-gather.13.cloned.1.call-done = bf16[1280,6,1280]{2,0,1:T(8,128)(2,1)} async-done(((bf16[320,6,1280]{2,0,1:T(8,128)(2,1)}), bf16[1280,6,1280]{2,0,1:T(8,128)(2,1)}) %all-gather.13.cloned.1.call-update) | async-done | bytes 19660816 | tf_op jit(solution)/shard_map/all_gather | solution.py:59
  175.4 27.7 %all-gather.17.cloned.1.call-done = bf16[1,1024,1280]{2,1,0:T(8,128)(2,1)} async-done(((bf16[1,256,1280]{2,1,0:T(8,128)(2,1)}), bf16[1,1024,1280]{2,1,0:T(8,128)(2,1)}) %all-gather.17.cloned.1.call-update) | async-done | bytes 2621456 | tf_op jit(solution)/shard_map/all_gather | solution.py:79
  231.6 13.7 %exponential_reduce_fusion = f32[16,384]{1,0:T(8,128)S(1)} fusion(f32[16,384,1152]{2,1,0:T(8,128)} %get-tuple-element.453, f32[16,384]{1,0:T(8,128)S(1)} %get-tuple-element.452, pred[384,1152]{1,0:T(8,128)(4,1)S(1)} %copy-done.3), kind=kLoop, calls=%fused_computation.3 | loop fusion | flops 21227520 | bytes 28803072 | tf_op jit(solution)/shard_map/reduce_sum | solution.py:107
  245.3 13.1 fusion.45
  289.8 24.5 %multiply_reduce_fusion = (f32[16,384]{1,0:T(8,128)S(1)}, f32[16,384,1152]{2,1,0:T(8,128)}) fusion(f32[16,384,1152]{2,1,0:T(8,128)} %get-tuple-element.453, f32[16,384]{1,0:T(8,128)S(1)} %log_add_fusion, pred[384,1152]{1,0:T(8,128)(4,1)} %fusion.44, bf16[384,16,80]{0,2,1:T(8,128)(2,1)} %bitcast.675, bf16[1152,16,80]{0,2,1:T(8,128)(2,1)} %bitcast.670), kind=kOutput, calls=%fused_computation.1 | convolution fusion | flops 1160767488 | bytes 61046784 | tf_op jit(solution)/shard_map/thd,khd->htk/dot_general | solution.py:139
  314.3 23.7 %multiply_convert_fusion = bf16[16,384,1152]{2,1,0:T(8,128)(2,1)} fusion(f32[16,384,1152]{2,1,0:T(8,128)} %get-tuple-element.458, f32[16,384,1152]{2,1,0:T(8,128)} %get-tuple-element.453, f32[16,384]{1,0:T(8,128)S(1)} %get-tuple-element.457, f32[16,384]{1,0:T(8,128)S(1)} %log_add_fusion, pred[384,1152]{1,0:T(8,128)(4,1)} %fusion.44), kind=kLoop, calls=%fused_computation | loop fusion | flops 35389440 | bytes 71270400 | tf_op jit(solution)/shard_map/convert_element_type | solution.py:141
  354.1 14.2 %fusion.9 = bf16[1152,16,80]{0,2,1:T(8,128)(2,1)S(1)} fusion(bf16[384,16,80]{0,2,1:T(8,128)(2,1)} %bitcast.676, f32[16,384,1152]{2,1,0:T(8,128)} %get-tuple-element.453, f32[16,384]{1,0:T(8,128)S(1)} %log_add_fusion, pred[384,1152]{1,0:T(8,128)(4,1)} %fusion.44), kind=kOutput, calls=%fused_computation.23 | convolution fusion | flops 1155170304 | bytes 32710656 | tf_op jit(solution)/shard_map/htk,thd->khd/dot_general | solution.py:142
  401.2 24.4 %reduce-scatter.11.cloned.1.call-done = bf16[256,1280]{1,0:T(8,128)(2,1)} async-done(((bf16[1024,1280]{1,0:T(8,128)(2,1)}), bf16[256,1280]{1,0:T(8,128)(2,1)}) %reduce-scatter.11.cloned.1.call-update) | async-done | bytes 655376 | tf_op jit(solution)/shard_map/reduce_scatter | solution.py:155
  442.1 17.9 %convolution_convert_fusion = bf16[6,1280,1280]{2,1,0:T(8,128)(2,1)} fusion(bf16[6,384,1280]{2,1,0:T(8,128)(2,1)} %get-tuple-element.460, bf16[6,384,1280]{2,1,0:T(8,128)(2,1)} %bitcast_dynamic-update-slice_fusion), kind=kOutput, calls=%fused_computation.4 | convolution fusion | flops 7559577600 | bytes 31457280 | tf_op jit(solution)/shard_map/mto,mti->omi/dot_general | solution.py:172
  460.0 26.4 %copy.101 = bf16[1280,7680]{1,0:T(8,128)(2,1)} copy(bf16[1280,7680]{0,1:T(8,128)(2,1)} %bitcast.674) | data formatting | bytes 39321600
  497.8 131.3 %reduce-scatter.13.cloned.1.call-done = bf16[320,7680]{1,0:T(8,128)(2,1)} async-done(((bf16[1280,7680]{1,0:T(8,128)(2,1)}), bf16[320,7680]{1,0:T(8,128)(2,1)}) %reduce-scatter.13.cloned.1.call-update) | async-done | bytes 4915216
  670.7 68.3 %all-reduce.3.cloned.1.call-done = (f32[320,8]{0,1:T(8,128)}, f32[320,8]{0,1:T(8,128)}, f32[320,8]{0,1:T(8,128)}, f32[320,8]{0,1:T(8,128)}, f32[320,8]{0,1:T(8,128)}, /*index=5*/f32[320,8]{0,1:T(8,128)}, f32[5,320]{1,0:T(8,128)}) async-done(((f32[320,8]{0,1:T(8,128)}, f32[320,8]{0,1:T(8,128)}, f32[320,8]{0,1:T(8,128)}, f32[320,8]{0,1:T(8,128)}, f32[320,8]{0,1:T(8,128)}, /*index=5*/f32[320,8]{0,1:T(8,128)}, ...) | async-done | bytes 67856 | tf_op jit(solution)/shard_map/psum | solution.py:198
  780.6 17.6 %subtract_multiply_fusion.35 = (f32[320,1,1]{0,2,1:T(1,128)S(1)}, f32[320,1,1]{0,2,1:T(1,128)S(1)}, f32[320,1,1]{0,2,1:T(1,128)S(1)}, f32[320,1,1]{0,2,1:T(1,128...) fusion(f32[320,1,1]{0,2,1:T(1,128)S(1)} %get-tuple-element.431, ...), kind=kLoop, calls=%fused_computation.616 | loop fusion | flops 20160 | bytes 19340 | tf_op jit(solution)/shard_map/mul | solution.py:32
  800.7 30.6 %all-gather.2 = bf16[10240,8]{0,1:T(8,128)(2,1)S(1)} all-gather(bf16[1280,8]{0,1:T(8,128)(2,1)S(1)} %convolution_convert_fusion.8), channel_id=4, replica_groups=mesh['rep'=8,'zero'=4] {'rep'}, dimensions={0}, use_global_device_ids=true | all-gather | bytes 184320 | tf_op jit(solution)/shard_map/all_gather | solution.py:204
  872.7 17.6 %subtract_multiply_fusion.28 = (f32[320,1,1]{0,2,1:T(1,128)S(1)}, f32[320,1,1]{0,2,1:T(1,128)S(1)}, f32[320,1,1]{0,2,1:T(1,128)S(1)}, f32[320,1,1]{0,2,1:T(1,128...) fusion(f32[320,1,1]{0,2,1:T(1,128)S(1)} %get-tuple-element.398, ...), kind=kLoop, calls=%fused_computation.560 | loop fusion | flops 20160 | bytes 19340 | tf_op jit(solution)/shard_map/mul | solution.py:32
  892.7 30.8 %all-gather.3 = bf16[10240,8]{0,1:T(8,128)(2,1)S(1)} all-gather(bf16[1280,8]{0,1:T(8,128)(2,1)S(1)} %convolution_convert_fusion.7), channel_id=5, replica_groups=mesh['rep'=8,'zero'=4] {'rep'}, dimensions={0}, use_global_device_ids=true | all-gather | bytes 184320 | tf_op jit(solution)/shard_map/all_gather | solution.py:204
  964.0 17.6 %subtract_multiply_fusion.21 = (f32[320,1,1]{0,2,1:T(1,128)S(1)}, f32[320,1,1]{0,2,1:T(1,128)S(1)}, f32[320,1,1]{0,2,1:T(1,128)S(1)}, f32[320,1,1]{0,2,1:T(1,128...) fusion(f32[320,1,1]{0,2,1:T(1,128)S(1)} %get-tuple-element.365, ...), kind=kLoop, calls=%fused_computation.504 | loop fusion | flops 20160 | bytes 19340 | tf_op jit(solution)/shard_map/mul | solution.py:32
  984.0 30.6 %all-gather.4 = bf16[10240,8]{0,1:T(8,128)(2,1)S(1)} all-gather(bf16[1280,8]{0,1:T(8,128)(2,1)S(1)} %convolution_convert_fusion.6), channel_id=6, replica_groups=mesh['rep'=8,'zero'=4] {'rep'}, dimensions={0}, use_global_device_ids=true | all-gather | bytes 184320 | tf_op jit(solution)/shard_map/all_gather | solution.py:204
  1055.5 17.6 %subtract_multiply_fusion.14 = (f32[320,1,1]{0,2,1:T(1,128)S(1)}, f32[320,1,1]{0,2,1:T(1,128)S(1)}, f32[320,1,1]{0,2,1:T(1,128)S(1)}, f32[320,1,1]{0,2,1:T(1,128...) fusion(f32[320,1,1]{0,2,1:T(1,128)S(1)} %get-tuple-element.332, ...), kind=kLoop, calls=%fused_computation.448 | loop fusion | flops 20160 | bytes 19340 | tf_op jit(solution)/shard_map/mul | solution.py:32
  1075.5 30.6 %all-gather.5 = bf16[10240,8]{0,1:T(8,128)(2,1)S(1)} all-gather(bf16[1280,8]{0,1:T(8,128)(2,1)S(1)} %convolution_convert_fusion.5), channel_id=7, replica_groups=mesh['rep'=8,'zero'=4] {'rep'}, dimensions={0}, use_global_device_ids=true | all-gather | bytes 184320 | tf_op jit(solution)/shard_map/all_gather | solution.py:204
  1146.9 17.5 %subtract_multiply_fusion.7 = (f32[320,1,1]{0,2,1:T(1,128)S(1)}, f32[320,1,1]{0,2,1:T(1,128)S(1)}, f32[320,1,1]{0,2,1:T(1,128)S(1)}, f32[320,1,1]{0,2,1:T(1,128)...) fusion(f32[320,1,1]{0,2,1:T(1,128)S(1)} %get-tuple-element.299, ...), kind=kLoop, calls=%fused_computation.392 | loop fusion | flops 20160 | bytes 19340 | tf_op jit(solution)/shard_map/mul | solution.py:32
  1166.8 30.6 %all-gather.6 = bf16[10240,8]{0,1:T(8,128)(2,1)S(1)} all-gather(bf16[1280,8]{0,1:T(8,128)(2,1)S(1)} %convolution_convert_fusion.4), channel_id=8, replica_groups=mesh['rep'=8,'zero'=4] {'rep'}, dimensions={0}, use_global_device_ids=true | all-gather | bytes 184320 | tf_op jit(solution)/shard_map/all_gather | solution.py:204
  1238.0 17.7 %subtract_multiply_fusion = (f32[320,1,1]{0,2,1:T(1,128)S(1)}, f32[320,1,1]{0,2,1:T(1,128)S(1)}, f32[320,1,1]{0,2,1:T(1,128)S(1)}, f32[320,1,1]{0,2,1:T(1,128)S(...) fusion(f32[320,1,1]{0,2,1:T(1,128)S(1)} %get-tuple-element.266, f32[]{:T(128)S(6)} %rsqrt.263, ...), kind=kLoop, calls=%fused_computation.336 | loop fusion | flops 20160 | bytes 19340 | tf_op jit(solution)/shard_map/mul | solution.py:32
  1258.1 30.9 %all-gather.7 = bf16[10240,8]{0,1:T(8,128)(2,1)S(1)} all-gather(bf16[1280,8]{0,1:T(8,128)(2,1)S(1)} %convolution_convert_fusion.3), channel_id=9, replica_groups=mesh['rep'=8,'zero'=4] {'rep'}, dimensions={0}, use_global_device_ids=true | all-gather | bytes 184320 | tf_op jit(solution)/shard_map/all_gather | solution.py:204
  (313 shorter events, 475.6 us)
Async XLA Ops:
  7.2 648.8 %copy-start = (f32[6,1280,8]{1,2,0:T(8,128)S(1)}, f32[6,1280,8]{1,2,0:T(8,128)}, u32[]{:S(2)}) copy-start(f32[6,1280,8]{1,2,0:T(8,128)} %param.14) | copy-start | bytes 737284
  7.2 129.4 %all-gather.13.cloned.1.call-start = ((), (), s32[]{:S(2)}) async-start(), calls=%async_computation.4 | async-start | bytes 24576000 | tf_op jit(solution)/shard_map/all_gather | solution.py:59
  7.9 167.5 %all-gather.15.cloned.1.call-start = ((), (), s32[]{:S(2)}) async-start(), calls=%async_computation.7 | async-start | bytes 3276800 | tf_op jit(solution)/shard_map/all_gather | solution.py:80
  14.3 132.7 %copy-start.25 = (f32[1280,5]{0,1:T(8,128)}, f32[1280,5]{0,1:T(8,128)S(1)}, u32[]{:S(2)}) copy-start(f32[1280,5]{0,1:T(8,128)S(1)} %reshape.8162) | copy-start | bytes 76804
  15.0 136.4 %copy-start.26 = (f32[1280]{0:T(1024)}, f32[1280]{0:T(1024)S(1)}, u32[]{:S(2)}) copy-start(f32[1280]{0:T(1024)S(1)} %get-tuple-element.55) | copy-start | bytes 15364
  15.0 138.7 %copy-start.22 = (f32[1280]{0:T(1024)}, f32[1280]{0:T(1024)S(1)}, u32[]{:S(2)}) copy-start(f32[1280]{0:T(1024)S(1)} %get-tuple-element.58) | copy-start | bytes 15364
  15.8 137.9 %copy-start.28 = (f32[384]{0:T(512)}, f32[384]{0:T(512)S(1)}, u32[]{:S(2)}) copy-start(f32[384]{0:T(512)S(1)} %get-tuple-element.447) | copy-start | bytes 4612
  149.7 53.4 %all-gather.17.cloned.1.call-start = ((), (), s32[]{:S(2)}) async-start(), calls=%async_computation.8 | async-start | bytes 3276800 | tf_op jit(solution)/shard_map/all_gather | solution.py:79
  150.5 248.2 %reduce-scatter.9.cloned.1.call-start = ((), (), s32[]{:S(2)}) async-start(), calls=%async_computation.5 | async-start | bytes 3276800 | tf_op jit(solution)/shard_map/reduce_scatter | solution.py:152
  218.6 13.1 copy-start.3
  231.6 13.7 %copy-start.2 = (bf16[1152,1280]{0,1:T(8,128)(2,1)S(1)}, bf16[1152,1280]{0,1:T(8,128)(2,1)}, u32[]{:S(2)}) copy-start(bf16[1152,1280]{0,1:T(8,128)(2,1)} %copy.80) | copy-start | bytes 8847364
  264.9 16.4 %copy-start.9 = (f32[384,1280]{1,0:T(8,128)}, f32[384,1280]{1,0:T(8,128)S(1)}, u32[]{:S(2)}) copy-start(f32[384,1280]{1,0:T(8,128)S(1)} %get-tuple-element.455) | copy-start | bytes 5898244
  354.0 71.6 %reduce-scatter.11.cloned.1.call-start = ((), (), s32[]{:S(2)}) async-start(), calls=%async_computation.6 | async-start | bytes 3276800 | tf_op jit(solution)/shard_map/reduce_scatter | solution.py:155
  376.2 119.9 %reduce-scatter.15.cloned.1.call-start = ((), (), s32[]{:S(2)}) async-start(), calls=%async_computation.10 | async-start | bytes 819200
  397.3 28.3 %copy-start.14 = (bf16[1,128,1280]{2,1,0:T(8,128)(2,1)S(1)}, bf16[1,128,1280]{2,1,0:T(8,128)(2,1)}, u32[]{:S(2)}) copy-start(bf16[1,128,1280]{2,1,0:T(8,128)(2,1)} %copy.88) | copy-start | bytes 983044
  398.7 29.2 %copy-start.6 = (f32[384,1280]{1,0:T(8,128)S(1)}, f32[384,1280]{1,0:T(8,128)}, u32[]{:S(2)}) copy-start(f32[384,1280]{1,0:T(8,128)} %copy-done.5) | copy-start | bytes 5898244
  442.1 187.0 %reduce-scatter.13.cloned.1.call-start = ((), (), s32[]{:S(2)}) async-start(), calls=%async_computation.9 | async-start | bytes 24576000
  486.4 252.5 %all-reduce.3.cloned.1.call-start = ((), (), s32[]{:S(2)}) async-start(), calls=%async_computation.11 | async-start | bytes 172032 | tf_op jit(solution)/shard_map/psum | solution.py:198
  739.0 184.6 %copy-start.34 = (f32[320,8]{0,1:T(8,128)S(1)}, f32[320,8]{0,1:T(8,128)}, u32[]{:S(2)}) copy-start(f32[320,8]{0,1:T(8,128)} %get-tuple-element.223) | copy-start | bytes 30724
  800.7 213.9 %copy-start.33 = (f32[320,8]{0,1:T(8,128)S(1)}, f32[320,8]{0,1:T(8,128)}, u32[]{:S(2)}) copy-start(f32[320,8]{0,1:T(8,128)} %get-tuple-element.224) | copy-start | bytes 30724
  892.7 213.4 %copy-start.32 = (f32[320,8]{0,1:T(8,128)S(1)}, f32[320,8]{0,1:T(8,128)}, u32[]{:S(2)}) copy-start(f32[320,8]{0,1:T(8,128)} %get-tuple-element.225) | copy-start | bytes 30724
  984.0 213.5 %copy-start.31 = (f32[320,8]{0,1:T(8,128)S(1)}, f32[320,8]{0,1:T(8,128)}, u32[]{:S(2)}) copy-start(f32[320,8]{0,1:T(8,128)} %get-tuple-element.226) | copy-start | bytes 30724
  1289.1 12.5 copy-start.16
  1289.2 12.5 copy-start.8
  (28 other events, 106.9 us)
Sparse Core Ops, SparseCore 0:
  9.6 126.9 all-gather.12
  149.9 25.5 all-gather.14
  177.6 25.5 all-gather.16
  354.1 34.4 reduce-scatter.8
  391.1 34.5 reduce-scatter.10
  442.2 22.4 reduce-scatter.14
  486.6 142.4 reduce-scatter.12
  667.5 71.4 all-reduce.2
